TPU v7x, 256 devices: a whole 4x4x8 slice. The times are simulated.
256 devices in a mesh: seq: 32 (over z, y), head: 8 (over x, core).
Axes of the slice: x: 4, y: 4, z: 8, core: 2. Of those that a mesh axis runs over, the one named last changes fastest.
Arguments:
- queries: bfloat16 [65536, 4096], P('seq', 'head'), may hold values from -6 to 6
- key_inputs: bfloat16 [65536, 4096], P('seq', 'head'), may hold values from -6 to 6
- values: bfloat16 [65536, 4096], P('seq', 'head'), may hold values from -36 to 36
- out_gain: float32 [4096], replicated, may hold values from 0.25 to 1.75
Outputs:
- normed: bfloat16 [65536, 4096], P(('seq', 'head'))
All inputs are finite; a program needn't handle non-finite values.
Results may differ from a plain program's by a relative error of at most 0.0056.
Values may be sent and summed in bfloat16 or wider, within the bound.
No kernel may reach another device: no remote copies, remote signals or barrier semaphores. Data moves between devices by JAX's collectives and lax.ppermute only.
A program may use at most 64 MiB of HBM per device.

v0:
```python
import jax
import jax.numpy as jnp
from jax import lax
from jax.sharding import PartitionSpec as P

HD = 128
BLOCK = 512


def shards(queries, key_inputs, values, out_gain):
    tok_rows = queries.shape[0]
    feature_count = queries.shape[1]
    local_heads = feature_count // HD
    block_count = tok_rows // BLOCK
    query_map = jax.nn.silu(queries.astype(jnp.float32)).astype(jnp.bfloat16)
    key_map = jax.nn.silu(key_inputs.astype(jnp.float32)).astype(jnp.bfloat16)
    query_map = query_map.reshape(block_count, BLOCK, local_heads, HD)
    key_map = key_map.reshape(block_count, BLOCK, local_heads, HD)
    value_blocks = values.reshape(block_count, BLOCK, local_heads, HD)
    block_states = jnp.einsum(
        "bshd,bshe->bhde", key_map, value_blocks, preferred_element_type=jnp.float32
    )
    running = jnp.cumsum(block_states, axis=0)
    earlier = jnp.concatenate([jnp.zeros_like(block_states[:1]), running[:-1]], axis=0)
    shard_state = running[-1]
    flat_state = shard_state.reshape(1, local_heads * HD * HD)
    slices = lax.all_to_all(flat_state, "seq", split_axis=1, concat_axis=0, tiled=True)
    slice_sums = jnp.cumsum(slices, axis=0)
    before = jnp.concatenate([jnp.zeros_like(slice_sums[:1]), slice_sums[:-1]], axis=0)
    returned = lax.all_to_all(before, "seq", split_axis=0, concat_axis=1, tiled=True)
    prefix = returned.reshape(local_heads, HD, HD)
    states = earlier + prefix[None]
    causal = jnp.tril(jnp.ones((BLOCK, BLOCK), dtype=bool))
    scores = jnp.einsum("bthd,bshd->bhts", query_map, key_map, preferred_element_type=jnp.float32)
    weights = jnp.where(causal[None, None], scores, 0.0).astype(jnp.bfloat16)
    inside = jnp.einsum(
        "bhts,bshd->bthd", weights, value_blocks, preferred_element_type=jnp.float32
    )
    carried = jnp.einsum(
        "bthd,bhde->bthe", query_map.astype(jnp.float32), states, precision=lax.Precision.HIGHEST
    )
    attended = (inside + carried).astype(jnp.bfloat16).reshape(tok_rows, feature_count)
    regrouped = lax.all_to_all(attended, "head", split_axis=0, concat_axis=1, tiled=True)
    wide_out = regrouped.astype(jnp.float32)
    mean_square = jnp.mean(wide_out * wide_out, axis=1, keepdims=True)
    return (wide_out * lax.rsqrt(mean_square + 1e-06) * out_gain).astype(jnp.bfloat16)


def solution(mesh):
    return jax.shard_map(
        shards,
        mesh=mesh,
        in_specs=(P("seq", "head"), P("seq", "head"), P("seq", "head"), P()),
        out_specs=P(("seq", "head"), None),
        check_vma=False,
    )
```

profile of v0, /device:TPU:1, one launch (start us, length us, event | category | flops | bytes accessed | tf_op | source)
XLA Modules:
  0.0 114.2 jit_solution(6354019923927095237)
XLA Ops:
  0.0 2.8 %fusion.7 = bf16[2048,512]{1,0:T(8,128)(2,1)S(1)} fusion(bf16[2048,512]{1,0:T(8,128)(2,1)} %param.5), kind=kLoop, calls=%fused_computation.14 | loop fusion | flops 6291456 | bytes 4194304 | tf_op jit(solution)/shard_map/convert_element_type | solution.py:16
  2.8 2.0 %reshape.48 = bf16[4,512,4,128]{3,2,1,0:T(4,128)(2,1)} reshape(bf16[2048,512]{1,0:T(8,128)(2,1)S(1)} %fusion.7) | data formatting | bytes 4194304 | tf_op jit(solution)/shard_map/reshape | solution.py:18
  4.8 3.0 %copy.32 = bf16[4,512,4,128]{1,3,2,0:T(8,128)(2,1)S(1)} copy(bf16[4,512,4,128]{3,2,1,0:T(4,128)(2,1)} %reshape.48) | data formatting | bytes 4194304 | tf_op jit(solution)/shard_map/reshape | solution.py:18
  7.7 4.0 %reshape.49 = bf16[4,512,4,128]{3,2,1,0:T(4,128)(2,1)} reshape(bf16[2048,512]{1,0:T(8,128)(2,1)} %param.6) | data formatting | bytes 4194304 | tf_op jit(solution)/shard_map/reshape | solution.py:19
  11.7 2.3 %fusion.13 = f32[4,4,128,128]{3,2,1,0:T(8,128)S(1)} fusion(bf16[4,512,4,128]{1,3,2,0:T(8,128)(2,1)S(1)} %copy.32, bf16[4,512,4,128]{3,2,1,0:T(4,128)(2,1)} %reshape.49), kind=kOutput, calls=%fused_computation.22 | convolution fusion | flops 268435456 | bytes 5242880 | tf_op jit(solution)/shard_map/bshd,bshe->bhde/dot_general | solution.py:20
  14.0 0.8 fusion.24
  14.8 0.8 slice.13
  15.6 12.0 %all-to-all-start = ((f32[1,32,2048]{2,0,1:T(1,128)}), f32[1,32,2048]{2,0,1:T(1,128)S(1)}, u32[]{:S(2)}, u32[]{:S(2)}) async-start(f32[1,32,2048]{2,0,1:T(1,128)} %bitcast.28), calls=%async_computation | async-start | bytes 524288 | tf_op jit(solution)/shard_map/all_to_all | solution.py:27
  27.6 4.1 %fusion.3 = bf16[2048,512]{1,0:T(8,128)(2,1)} fusion(bf16[2048,512]{1,0:T(8,128)(2,1)} %param.4), kind=kLoop, calls=%fused_computation.10 | loop fusion | flops 6291456 | bytes 4194304 | tf_op jit(solution)/shard_map/convert_element_type | solution.py:15
  31.7 4.0 %reshape.47 = bf16[4,512,4,128]{3,2,1,0:T(4,128)(2,1)} reshape(bf16[2048,512]{1,0:T(8,128)(2,1)} %fusion.3) | data formatting | bytes 4194304 | tf_op jit(solution)/shard_map/reshape | solution.py:17
  35.7 0.8 iota_compare_fusion
  36.5 2.4 %all-to-all-done = f32[1,32,2048]{2,0,1:T(1,128)S(1)} async-done(((f32[1,32,2048]{2,0,1:T(1,128)}), f32[1,32,2048]{2,0,1:T(1,128)S(1)}, u32[]{:S(2)}, u32[]{:S(2)}) %all-to-all-start) | async-done | bytes 262176 | tf_op jit(solution)/shard_map/all_to_all | solution.py:27
  39.3 1.0 copy.35
  40.3 7.0 %all-to-all-start.1 = ((f32[32,1,2048]{2,1,0:T(1,128)}), f32[32,1,2048]{2,1,0:T(1,128)S(1)}, u32[]{:S(2)}, u32[]{:S(2)}) async-start(f32[32,1,2048]{2,1,0:T(1,128)} %copy.35), calls=%async_computation.1 | async-start | bytes 524288 | tf_op jit(solution)/shard_map/all_to_all | solution.py:30
  47.2 8.8 %fusion.12 = f32[4,4,512,128]{3,2,1,0:T(8,128)} fusion(bf16[4,512,4,128]{1,3,2,0:T(8,128)(2,1)S(1)} %copy.32, pred[512,512]{1,0:T(8,128)(4,1)S(1)} %copy-done.1, bf16[4,512,4,128]{3,2,1,0:T(4,128)(2,1)} %reshape.49, bf16[4,512,4,128]{3,2,1,0:T(4,128)(2,1)} %reshape.47), kind=kOutput, calls=%fused_computation.21 | convolution fusion | flops 2155872256 | bytes 10747904 | tf_op jit(solution)/shard_map/bhts,bshd->bthd/dot_general | solution.py:36
  56.0 1.7 %all-to-all-done.1 = f32[32,1,2048]{2,1,0:T(1,128)S(1)} async-done(((f32[32,1,2048]{2,1,0:T(1,128)}), f32[32,1,2048]{2,1,0:T(1,128)S(1)}, u32[]{:S(2)}, u32[]{:S(2)}) %all-to-all-start.1) | async-done | bytes 262176 | tf_op jit(solution)/shard_map/all_to_all | solution.py:30
  57.7 4.9 %fusion.11 = bf16[4,512,4,128]{3,1,2,0:T(8,128)(2,1)S(1)} fusion(f32[4,4,512,128]{3,2,1,0:T(8,128)} %fusion.12, bf16[4,512,4,128]{3,2,1,0:T(4,128)(2,1)} %reshape.47, f32[3,4,128,128]{3,2,1,0:T(8,128)S(1)} %slice-done, f32[4,128,128]{2,1,0:T(8,128)S(1)} %bitcast.25), kind=kOutput, calls=%fused_computation.20 | convolution fusion | flops 1612972032 | bytes 9437184 | tf_op jit(solution)/shard_map/bthd,bhde->bthe/dot_general | solution.py:39
  62.6 1.6 %copy.39 = bf16[4,512,4,128]{3,2,1,0:T(4,128)(2,1)S(1)} copy(bf16[4,512,4,128]{3,1,2,0:T(8,128)(2,1)S(1)} %fusion.11) | data formatting | bytes 4194304 | tf_op jit(solution)/shard_map/convert_element_type | solution.py:42
  64.2 2.2 %all_to_all.37 = bf16[8,256,512]{2,1,0:T(8,128)(2,1)} reshape(bf16[4,512,4,128]{3,2,1,0:T(4,128)(2,1)S(1)} %copy.39) | data formatting | bytes 4194304 | tf_op jit(solution)/shard_map/all_to_all | solution.py:43
  66.4 33.7 %all_to_all.42 = bf16[8,256,512]{2,1,0:T(8,128)(2,1)S(1)} all-to-all(bf16[8,256,512]{2,1,0:T(8,128)(2,1)} %all_to_all.37), channel_id=1, replica_groups=mesh['seq'=32,'head'=8] {'head'}, dimensions={0} | all-to-all | bytes 4194304 | tf_op jit(solution)/shard_map/all_to_all | solution.py:43
  100.1 2.5 %convert_bitcast_fusion = f32[256,8,512]{2,0,1:T(8,128)} fusion(bf16[8,256,512]{2,1,0:T(8,128)(2,1)S(1)} %all_to_all.42), kind=kLoop, calls=%fused_computation.2 | loop fusion | flops 1048576 | bytes 6291456 | tf_op jit(solution)/shard_map/convert_element_type | solution.py:44
  102.6 5.4 %copy.40 = f32[256,8,512]{0,2,1:T(8,128)} copy(f32[256,8,512]{2,0,1:T(8,128)} %convert_bitcast_fusion) | data formatting | bytes 8388608 | tf_op jit(solution)/shard_map/convert_element_type | solution.py:44
  108.7 2.6 %fusion.10 = bf16[256,4096]{0,1:T(8,128)(2,1)S(1)} fusion(f32[256,8,512]{0,2,1:T(8,128)} %copy.40, f32[4096]{0:T(1024)S(1)} %copy-done.2, f32[256]{0:T(256)S(1)} %add_rsqrt_fusion), kind=kLoop, calls=%fused_computation.18 | loop fusion | flops 3145728 | bytes 6308864 | tf_op jit(solution)/shard_map/convert_element_type | solution.py:46
  111.3 2.9 %copy.41 = bf16[256,4096]{1,0:T(8,128)(2,1)} copy(bf16[256,4096]{0,1:T(8,128)(2,1)S(1)} %fusion.10) | data formatting | bytes 4194304 | tf_op jit(solution)/shard_map/convert_element_type | solution.py:46
  (13 shorter events, 1.1 us)
Async XLA Ops:
  14.8 16.9 %copy-start = (f32[4,4,128,128]{3,2,1,0:T(8,128)}, f32[4,4,128,128]{3,2,1,0:T(8,128)S(1)}, u32[]{:S(2)}) copy-start(f32[4,4,128,128]{3,2,1,0:T(8,128)S(1)} %fusion.24) | copy-start | bytes 3145732
  15.6 23.3 %all-to-all-start = ((f32[1,32,2048]{2,0,1:T(1,128)}), f32[1,32,2048]{2,0,1:T(1,128)S(1)}, u32[]{:S(2)}, u32[]{:S(2)}) async-start(f32[1,32,2048]{2,0,1:T(1,128)} %bitcast.28), calls=%async_computation | async-start | bytes 524288 | tf_op jit(solution)/shard_map/all_to_all | solution.py:27
  39.0 8.2 %copy-start.1 = (pred[512,512]{1,0:T(8,128)(4,1)S(1)}, pred[512,512]{1,0:T(8,128)(4,1)}, u32[]{:S(2)}) copy-start(pred[512,512]{1,0:T(8,128)(4,1)} %iota_compare_fusion) | copy-start | bytes 786436
  40.3 17.4 %all-to-all-start.1 = ((f32[32,1,2048]{2,1,0:T(1,128)}), f32[32,1,2048]{2,1,0:T(1,128)S(1)}, u32[]{:S(2)}, u32[]{:S(2)}) async-start(f32[32,1,2048]{2,1,0:T(1,128)} %copy.35), calls=%async_computation.1 | async-start | bytes 524288 | tf_op jit(solution)/shard_map/all_to_all | solution.py:30
  47.2 10.5 %slice-start = ((f32[4,4,128,128]{3,2,1,0:T(8,128)}), f32[3,4,128,128]{3,2,1,0:T(8,128)S(1)}, s32[]{:S(2)}) async-start(f32[4,4,128,128]{3,2,1,0:T(8,128)} %copy-done), calls=%async_computation.3 | async-start | bytes 1572864 | tf_op jit(solution)/shard_map/slice | solution.py:24
  108.0 0.7 copy-start.2
where the time goes:
time: 115 us; the launch traced here: 114 us
  blocking collectives  33.7 us (29%)
  local copies, waits for them, and re-layouts  27.1 us (24%)
  starting transfers between devices  19 us (17%)
  matrix products  16 us (14%)
  other arithmetic  14.3 us (12%)
  waiting for transfers between devices  4.13 us (4%)
    all_to_all x1, blocking collectives, shards(): lax.all_to_all(attended, 'head', split_axis=0, concat_axis=1, tiled=True)  33.7 us
    all_to_all x1, starting transfers between devices, shards(): lax.all_to_all(flat_state, 'seq', split_axis=1, concat_axis=0, tiled=True)  12 us
    dot_general x1, matrix products, shards(): jnp.einsum('bhts,bshd->bthd', weights, value_blocks, preferred_element_ty...  8.76 us
    all_to_all x1, starting transfers between devices, shards(): lax.all_to_all(before, 'seq', split_axis=0, concat_axis=1, tiled=True)  6.95 us
    convert_element_type x1, local copies, waits for them, and re-layouts, shards(): wide_out = regrouped.astype(jnp.float32)  5.36 us
    reshape x2, local copies, waits for them, and re-layouts, shards(): key_map = key_map.reshape(block_count, BLOCK, local_heads, HD)  4.99 us
    dot_general x1, matrix products, shards(): jnp.einsum('bthd,bhde->bthe', query_map.astype(jnp.float32), states, prec...  4.92 us
    convert_element_type x1, other arithmetic, shards(): query_map = jax.nn.silu(queries.astype(jnp.float32)).astype(jnp.bfloat16)  4.1 us
  transfers between devices with their start and end apart: 2, of which 2 were waited for; matrix products, arithmetic and copies ran while one was open for 15% of the time, Pallas kernels for 0%

commit v1 on v0

v1 whole, which is shorter than its diff:
```python
import jax
import jax.numpy as jnp
from jax import lax
from jax.experimental import pallas as pl
from jax.experimental.pallas import tpu as pltpu
from jax.sharding import PartitionSpec as P

HD = 128
BLOCK = 512
F32 = jnp.float32
BF16 = jnp.bfloat16
WHOLE = pl.BlockSpec(memory_space=pltpu.VMEM)
SCALAR = pl.BlockSpec(memory_space=pltpu.SMEM)
PARAMS = pltpu.CompilerParams(vmem_limit_bytes=24 * 1024 * 1024)


def near(x):
    return pltpu.with_memory_space_constraint(x, pltpu.VMEM)


def far(x):
    return pltpu.with_memory_space_constraint(x, pltpu.HBM)


def silu(u):
    half = 0.5 * u.astype(F32)
    return (half + half * jnp.tanh(half)).astype(BF16)


def state_kernel(k_ref, v_ref, local_ref, total_ref):
    b = pl.program_id(0)

    @pl.when(b == 0)
    def _():
        total_ref[...] = jnp.zeros_like(total_ref)

    local_ref[0] = total_ref[...]
    for h in range(total_ref.shape[0]):
        cols = slice(h * HD, (h + 1) * HD)
        key_map = silu(k_ref[:, cols])
        total_ref[h] += lax.dot_general(
            key_map, v_ref[:, cols], (((0,), (0,)), ((), ())), preferred_element_type=F32
        )


def shard_states(k, v):
    rows, feats = k.shape
    heads = feats // HD
    blocks = rows // BLOCK
    spec = pl.BlockSpec((BLOCK, feats), lambda b: (b, 0))
    return pl.pallas_call(
        state_kernel,
        grid=(blocks,),
        in_specs=[spec, spec],
        out_specs=[
            pl.BlockSpec((1, heads, HD, HD), lambda b: (b, 0, 0, 0)),
            pl.BlockSpec((heads, HD, HD), lambda b: (0, 0, 0)),
        ],
        out_shape=[pltpu.HBM((blocks, heads, HD, HD), F32), pltpu.HBM((heads, HD, HD), F32)],
        compiler_params=PARAMS,
        name="states",
    )(far(k), far(v))


def inside_kernel(q_ref, k_ref, v_ref, out_ref, qm_ref):
    half = BLOCK // 2
    row = lax.broadcasted_iota(jnp.int32, (half, half), 0)
    col = lax.broadcasted_iota(jnp.int32, (half, half), 1)
    causal = row >= col
    nt = (((1,), (1,)), ((), ()))
    for h in range(q_ref.shape[1] // HD):
        cols = slice(h * HD, (h + 1) * HD)
        qm = silu(q_ref[:, cols])
        km = silu(k_ref[:, cols])
        vv = v_ref[:, cols]
        qm_ref[:, cols] = qm
        for t in range(2):
            rows = slice(t * half, (t + 1) * half)
            diag = lax.dot_general(qm[rows], km[rows], nt, preferred_element_type=F32)
            diag = jnp.where(causal, diag, 0.0).astype(BF16)
            acc = jnp.dot(diag, vv[rows], preferred_element_type=F32)
            if t == 1:
                past = lax.dot_general(qm[rows], km[:half], nt, preferred_element_type=F32).astype(BF16)
                acc = acc + jnp.dot(past, vv[:half], preferred_element_type=F32)
            out_ref[rows, cols] = acc


def inside_part(q, k, v, part, parts):
    rows, feats = q.shape
    feats = feats // parts
    blocks = rows // BLOCK
    spec = pl.BlockSpec((BLOCK, feats), lambda b: (b, part))
    return pl.pallas_call(
        inside_kernel,
        grid=(blocks,),
        in_specs=[spec, spec, spec],
        out_specs=[pl.BlockSpec((BLOCK, feats), lambda b: (b, 0))] * 2,
        out_shape=[pltpu.HBM((rows, feats), F32), pltpu.HBM((rows, feats), BF16)],
        compiler_params=PARAMS,
        name="inside",
    )(far(q), far(k), far(v))


def scan_kernel(x_ref, o_ref):
    run = jnp.zeros(x_ref.shape[1:], F32)
    for s in range(x_ref.shape[0]):
        o_ref[s] = run
        run = run + x_ref[s]


def scan_slices(x):
    return pl.pallas_call(
        scan_kernel,
        in_specs=[WHOLE],
        out_specs=pl.BlockSpec(x.shape, lambda: (0, 0, 0)),
        out_shape=pltpu.HBM(x.shape, F32),
        compiler_params=PARAMS,
        name="scan",
    )(near(x))


def carried_kernel(shifts, size, parts, me_ref, *refs):
    inside_refs, qm_refs = refs[:parts], refs[parts : 2 * parts]
    local_ref, prefix_ref = refs[2 * parts : 2 * parts + 2]
    out_refs = refs[2 * parts + 2 : -4]
    inside_buf, qm_buf, local_buf, sems = refs[-4:]
    count = out_refs[0].shape[0]
    per_part = prefix_ref.shape[0] // parts

    def copies(i):
        dest = lax.rem(me_ref[0] + shifts[i], size)
        rows = pl.ds(pl.multiple_of(dest * count, count), count)
        moves = [(local_ref.at[dest * count // BLOCK], local_buf.at[i])]
        for p in range(parts):
            moves.append((inside_refs[p].at[rows], inside_buf.at[i, p]))
            moves.append((qm_refs[p].at[rows], qm_buf.at[i, p]))
        return [pltpu.make_async_copy(a, b, sems.at[i, n]) for n, (a, b) in enumerate(moves)]

    for i in range(len(shifts)):
        for move in copies(i):
            move.start()
    for i, out_ref in enumerate(out_refs):
        for move in copies(i):
            move.wait()
        for h in range(prefix_ref.shape[0]):
            part, at = divmod(h, per_part)
            cols = slice(at * HD, (at + 1) * HD)
            state = local_buf[i, h] + prefix_ref[h]
            acc = inside_buf[i, part, :, cols]
            qm = qm_buf[i, part, :, cols]
            for _ in range(3):
                piece = state.astype(BF16)
                state = state - piece.astype(F32)
                acc = acc + jnp.dot(qm, piece, preferred_element_type=F32)
            out_ref[:, h * HD : (h + 1) * HD] = acc.astype(BF16)


def carried_rows(shifts, size, me, inside, qm, local, prefix):
    parts = len(inside)
    count = inside[0].shape[0] // size
    width = inside[0].shape[1]
    n = len(shifts)

    def kernel(*refs):
        carried_kernel(shifts, size, parts, *refs)

    return pl.pallas_call(
        kernel,
        in_specs=[SCALAR] + [pl.BlockSpec(memory_space=pl.ANY)] * (2 * parts + 1) + [WHOLE],
        out_specs=[WHOLE] * n,
        out_shape=[pltpu.VMEM((count, width * parts), BF16)] * n,
        scratch_shapes=[
            pltpu.VMEM((n, parts, count, width), F32),
            pltpu.VMEM((n, parts, count, width), BF16),
            pltpu.VMEM((n,) + local.shape[1:], F32),
            pltpu.SemaphoreType.DMA((n, 2 * parts + 1)),
        ],
        compiler_params=PARAMS,
        name="carried",
    )(me, *[far(x) for x in (*inside, *qm, local)], near(prefix))


def norm_kernel(shifts, step, me_ref, gain_ref, *refs):
    parts, out_ref = refs[:-1], refs[-1]
    feats = parts[0].shape[1]
    size = len(shifts)
    rows = pl.ds(pl.program_id(0) * step, step)
    total = None
    for part in parts:
        wide = part[rows].astype(F32)
        total = wide * wide if total is None else total + wide * wide
    mean = jnp.sum(total, axis=1, keepdims=True) * (1.0 / out_ref.shape[1])
    scale = lax.rsqrt(mean + 1e-06)
    for shift, part in zip(shifts, parts):
        src = lax.rem(me_ref[0] + (size - shift), size)
        at = pl.ds(pl.multiple_of(src * feats, feats), feats)
        out_ref[:, at] = (part[rows].astype(F32) * scale * gain_ref[:, at]).astype(BF16)


def norm_rows(shifts, me, gain, parts):
    rows, feats = parts[0].shape
    n = len(parts)
    step = 64

    def kernel(*refs):
        norm_kernel(shifts, step, *refs)

    return pl.pallas_call(
        kernel,
        grid=(rows // step,),
        in_specs=[SCALAR] + [WHOLE] * (n + 1),
        out_specs=pl.BlockSpec((step, n * feats), lambda i: (i, 0)),
        out_shape=jax.ShapeDtypeStruct((rows, n * feats), BF16),
        compiler_params=PARAMS,
        name="norm",
    )(me, gain, *[near(p) for p in parts])


def shards(queries, key_inputs, values, out_gain, seq_size, head_size):
    _, feats = queries.shape
    heads = feats // HD
    me = lax.axis_index("head").astype(jnp.int32).reshape(1)
    local, total = shard_states(key_inputs, values)
    slices = total.reshape(seq_size, heads * HD // seq_size, HD)
    slices = lax.all_to_all(slices, "seq", 0, 0, tiled=True)
    inside_a, qm_a = inside_part(queries, key_inputs, values, 0, 2)
    before = scan_slices(slices)
    prefix = lax.all_to_all(before, "seq", 0, 0, tiled=True)
    inside_b, qm_b = inside_part(queries, key_inputs, values, 1, 2)
    prefix = prefix.reshape(heads, HD, HD)
    order = [d for k in range(head_size // 2, 0, -1) for d in dict.fromkeys((k, head_size - k))] + [0]
    groups = [order[:1], order[1:3], order[3:]]
    parts = []
    inside, qm = (inside_a, inside_b), (qm_a, qm_b)
    for shifts in groups:
        out = carried_rows(tuple(shifts), head_size, me, inside, qm, local, prefix)
        for d, rows_out in zip(shifts, out):
            if d:
                rows_out = lax.ppermute(rows_out, "head", [(i, (i + d) % head_size) for i in range(head_size)])
            parts.append(rows_out)
    return norm_rows(tuple(order), me, out_gain.reshape(1, -1), parts)


def solution(mesh):
    seq_size, head_size = mesh.shape["seq"], mesh.shape["head"]

    def run(queries, key_inputs, values, out_gain):
        return shards(queries, key_inputs, values, out_gain, seq_size, head_size)

    return jax.shard_map(
        run,
        mesh=mesh,
        in_specs=(P("seq", "head"), P("seq", "head"), P("seq", "head"), P()),
        out_specs=P(("seq", "head"), None),
        check_vma=False,
    )
```

time: 115 us -> 77.5 us (0.67)
  Pallas kernels: 0 us -> 27.1 us
  local copies, waits for them, and re-layouts: 27.1 us -> 0.01 us
  matrix products: 16 us -> 0 us
  other arithmetic: 14.3 us -> 0 us
  blocking collectives: 33.7 us -> 23.3 us
  waiting for transfers between devices: 4.13 us -> 9.94 us
  starting transfers between devices: 19 us -> 16.5 us
    pallas_call x0 -> x8, Pallas kernels: none -> 27.1 us  [the longest x2 12 us: inside_part(): pl.pallas_call(inside_kernel, grid=(blocks,), in_specs=[spec, spec, spec]...]
    dot_general x3 -> x0, matrix products: 16 us -> none  [the longest x1 8.76 us: shards(): jnp.einsum('bhts,bshd->bthd', weights, value_blocks, preferred_element_ty...]
    all_to_all x2 -> x1, starting transfers between devices: 19 us -> 4.7 us  [shards(): prefix = lax.all_to_all(before, 'seq', 0, 0, tiled=True)]
    reshape x4 -> x0, local copies, waits for them, and re-layouts: 12.9 us -> none  [the longest x2 4.99 us: shards(): key_map = key_map.reshape(block_count, BLOCK, local_heads, HD)]
    convert_element_type x4 -> x0, other arithmetic: 12 us -> none  [the longest x1 4.1 us: shards(): query_map = jax.nn.silu(queries.astype(jnp.float32)).astype(jnp.bfloat16)]
    ppermute x0 -> x7, starting transfers between devices: none -> 11.8 us  [shards(): lax.ppermute(rows_out, 'head', [(i, (i + d) % head_size) for i in range(h...]
    all_to_all x1, blocking collectives: 33.7 us -> 23.3 us  [shards(): slices = lax.all_to_all(slices, 'seq', 0, 0, tiled=True)]
    ppermute x0 -> x7, waiting for transfers between devices: none -> 9.94 us  [shards(): lax.ppermute(rows_out, 'head', [(i, (i + d) % head_size) for i in range(h...]
  transfers between devices with their start and end apart: 2 -> 8, of which waited for: 2 -> 4; matrix products, arithmetic and copies ran while one was open for 15% -> 0% of each run, Pallas kernels for 0% -> 23%
where the time goes in v1:
time: 77.5 us; the launch traced here: 76.9 us
  Pallas kernels  27.1 us (35%)
  blocking collectives  23.3 us (30%)
  starting transfers between devices  16.5 us (21%)
  waiting for transfers between devices  9.94 us (13%)
    all_to_all x1, blocking collectives, shards(): slices = lax.all_to_all(slices, 'seq', 0, 0, tiled=True)  23.3 us
    pallas_call x2, Pallas kernels, inside_part(): pl.pallas_call(inside_kernel, grid=(blocks,), in_specs=[spec, spec, spec]...  12 us
    ppermute x7, starting transfers between devices, shards(): lax.ppermute(rows_out, 'head', [(i, (i + d) % head_size) for i in range(h...  11.8 us
    ppermute x7, waiting for transfers between devices, shards(): lax.ppermute(rows_out, 'head', [(i, (i + d) % head_size) for i in range(h...  9.94 us
    pallas_call x3, Pallas kernels, carried_rows(): pl.pallas_call(kernel, in_specs=[SCALAR] + [pl.BlockSpec(memory_space=pl....  7.2 us
    all_to_all x1, starting transfers between devices, shards(): prefix = lax.all_to_all(before, 'seq', 0, 0, tiled=True)  4.7 us
    pallas_call x1, Pallas kernels, shard_states(): pl.pallas_call(state_kernel, grid=(blocks,), in_specs=[spec, spec], out_s...  4.7 us
    pallas_call x1, Pallas kernels, norm_rows(): pl.pallas_call(kernel, grid=(rows // step,), in_specs=[SCALAR] + [WHOLE]...  2.46 us
  transfers between devices with their start and end apart: 8, of which 4 were waited for; matrix products, arithmetic and copies ran while one was open for 0% of the time, Pallas kernels for 23%

profile of v1, /device:TPU:1, one launch (start us, length us, event | category | flops | bytes accessed | tf_op | source)
XLA Modules:
  0.0 76.9 jit_solution(1999915931285053782)
XLA Ops:
  0.0 4.7 %states.1 = (f32[4,4,128,128]{3,2,1,0:T(8,128)}, f32[4,128,128]{2,1,0:T(8,128)}) custom-call(bf16[2048,512]{1,0:T(8,128)(2,1)} %k_ref.5, bf16[2048,512]{1,0:T(8,128)(2,1)} %v_ref.5), custom_call_target="tpu_custom_call" | custom-call | tf_op jit(solution)/shard_map/states/pallas_call | solution.py:51
  4.7 23.3 %all_to_all.10.x_ref = f32[32,16,128]{2,1,0:T(8,128)S(1)} all-to-all(f32[32,16,128]{2,1,0:T(8,128)} %bitcast.8), channel_id=1, replica_groups=mesh['seq'=32,'head'=8] {'seq'}, dimensions={0} | all-to-all | bytes 524288 | tf_op jit(solution)/shard_map/all_to_all | solution.py:225
  28.0 0.8 scan.1
  28.8 4.7 %all-to-all-start.1 = ((f32[32,16,128]{2,1,0:T(8,128)}), f32[32,16,128]{2,1,0:T(8,128)S(1)}, u32[]{:S(2)}, u32[]{:S(2)}) async-start(f32[32,16,128]{2,1,0:T(8,128)} %scan.1), calls=%async_computation.1 | async-start | bytes 524288 | tf_op jit(solution)/shard_map/all_to_all | solution.py:228
  33.5 6.0 %inside.2 = (f32[2048,256]{1,0:T(8,128)}, bf16[2048,256]{1,0:T(8,128)(2,1)}) custom-call(bf16[2048,512]{1,0:T(8,128)(2,1)} %q_ref.3, bf16[2048,512]{1,0:T(8,128)(2,1)} %k_ref.5, bf16[2048,512]{1,0:T(8,128)(2,1)} %v_ref.5), custom_call_target="tpu_custom_call" | custom-call | tf_op jit(solution)/shard_map/inside/pallas_call | solution.py:93
  39.5 6.0 %inside.3 = (f32[2048,256]{1,0:T(8,128)}, bf16[2048,256]{1,0:T(8,128)(2,1)}) custom-call(bf16[2048,512]{1,0:T(8,128)(2,1)} %q_ref.3, bf16[2048,512]{1,0:T(8,128)(2,1)} %k_ref.5, bf16[2048,512]{1,0:T(8,128)(2,1)} %v_ref.5), custom_call_target="tpu_custom_call" | custom-call | tf_op jit(solution)/shard_map/inside/pallas_call | solution.py:93
  45.5 0.0 all-to-all-done.1
  45.5 1.6 %carried.3 = bf16[256,512]{1,0:T(8,128)(2,1)S(1)} custom-call(s32[1]{0:T(128)} %bitcast.refs_0_, f32[2048,256]{1,0:T(8,128)} %get-tuple-element.18.refs_1_, f32[2048,256]{1,0:T(8,128)} %get-tuple-element.19.refs_2_, bf16[2048,256]{1,0:T(8,128)(2,1)} %get-tuple-element.20.refs_3_, bf16[2048,256]{1,0:T(8,128)(2,1)} %get-tuple-element.21.refs_4_, ...), custom_call_target="tpu_custom_call" | custom-call | tf_op jit(solution)/shard_map/carried/pallas_call | solution.py:167
  47.1 2.8 %collective-permute-start = (bf16[256,512]{1,0:T(8,128)(2,1)S(1)}, bf16[256,512]{1,0:T(8,128)(2,1)S(1)}, u32[]{:S(2)}, u32[]{:S(2)}) collective-permute-start(bf16[256,512]{1,0:T(8,128)(2,1)S(1)} %carried.3), channel_id=1, source_target_pairs={{0,4},{1,5},{2,6},{3,7},{4,0},{5,1},{6,2},{7,3},{8,12},{9,13},{10,... | collective-permute-start | bytes 786440 | tf_op jit(solution)/shard_map/ppermute | solution.py:239
  49.9 2.0 %carried.4 = (bf16[256,512]{1,0:T(8,128)(2,1)S(1)}, bf16[256,512]{1,0:T(8,128)(2,1)S(1)}) custom-call(s32[1]{0:T(128)} %bitcast.refs_0_, f32[2048,256]{1,0:T(8,128)} %get-tuple-element.18.refs_1_, f32[2048,256]{1,0:T(8,128)} %get-tuple-element.19.refs_2_, bf16[2048,256]{1,0:T(8,128)(2,1)} %get-tuple-element.20.refs_3_, ...), custom_call_target="tpu_custom_call" | custom-call | tf_op jit(solution)/shard_map/carried/pallas_call | solution.py:167
  52.0 0.0 copy-start
  52.0 2.6 %collective-permute-start.1 = (bf16[256,512]{1,0:T(8,128)(2,1)S(1)}, bf16[256,512]{1,0:T(8,128)(2,1)S(1)}, u32[]{:S(2)}, u32[]{:S(2)}) collective-permute-start(bf16[256,512]{1,0:T(8,128)(2,1)S(1)} %get-tuple-element.24), channel_id=1, source_target_pairs={{0,3},{1,4},{2,5},{3,6},{4,7},{5,0},{6,1},{7,2},{8,11},{9,12},{10,... | collective-permute-start | bytes 786440 | tf_op jit(solution)/shard_map/ppermute | solution.py:239
  54.6 3.6 %carried.5 = (bf16[256,512]{1,0:T(8,128)(2,1)S(1)}, bf16[256,512]{1,0:T(8,128)(2,1)S(1)}, bf16[256,512]{1,0:T(8,128)(2,1)S(1)}, bf16[256,512]{1,0:T(8,128)(2,1)S(1)}, bf16[256,512]{1,0:T(8,128)(2,1)S(1)}) custom-call(s32[1]{0:T(128)} %bitcast.refs_0_, f32[2048,256]{1,0:T(8,128)} %get-tuple-element.18.refs_1_, f32[2048,256]{1,0:T(8,128)} %get-tuple-element.19.refs_2_, ...), custom_call_target="tpu_custom_call" | custom-call | tf_op jit(solution)/shard_map/carried/pallas_call | solution.py:167
  58.2 0.5 collective-permute-start.2
  58.6 0.9 %collective-permute-start.3 = (bf16[256,512]{1,0:T(8,128)(2,1)S(1)}, bf16[256,512]{1,0:T(8,128)(2,1)S(1)}, u32[]{:S(2)}, u32[]{:S(2)}) collective-permute-start(bf16[256,512]{1,0:T(8,128)(2,1)S(1)} %get-tuple-element.26), channel_id=1, source_target_pairs={{0,2},{1,3},{2,4},{3,5},{4,6},{5,7},{6,0},{7,1},{8,10},{9,11},{10,... | collective-permute-start | bytes 786440 | tf_op jit(solution)/shard_map/ppermute | solution.py:239
  59.6 1.7 %collective-permute-start.4 = (bf16[256,512]{1,0:T(8,128)(2,1)S(1)}, bf16[256,512]{1,0:T(8,128)(2,1)S(1)}, u32[]{:S(2)}, u32[]{:S(2)}) collective-permute-start(bf16[256,512]{1,0:T(8,128)(2,1)S(1)} %get-tuple-element.27), channel_id=1, source_target_pairs={{0,6},{1,7},{2,0},{3,1},{4,2},{5,3},{6,4},{7,5},{8,14},{9,15},{10,... | collective-permute-start | bytes 786440 | tf_op jit(solution)/shard_map/ppermute | solution.py:239
  61.3 0.0 collective-permute-done.refs_2_
  61.3 2.4 %collective-permute-start.5 = (bf16[256,512]{1,0:T(8,128)(2,1)S(1)}, bf16[256,512]{1,0:T(8,128)(2,1)S(1)}, u32[]{:S(2)}, u32[]{:S(2)}) collective-permute-start(bf16[256,512]{1,0:T(8,128)(2,1)S(1)} %get-tuple-element.28), channel_id=1, source_target_pairs={{0,1},{1,2},{2,3},{3,4},{4,5},{5,6},{6,7},{7,0},{8,9},{9,10},{10,1... | collective-permute-start | bytes 786440 | tf_op jit(solution)/shard_map/ppermute | solution.py:239
  63.7 0.8 %collective-permute-start.6 = (bf16[256,512]{1,0:T(8,128)(2,1)S(1)}, bf16[256,512]{1,0:T(8,128)(2,1)S(1)}, u32[]{:S(2)}, u32[]{:S(2)}) collective-permute-start(bf16[256,512]{1,0:T(8,128)(2,1)S(1)} %get-tuple-element.29), channel_id=1, source_target_pairs={{0,7},{1,0},{2,1},{3,2},{4,3},{5,4},{6,5},{7,6},{8,15},{9,8},{10,9... | collective-permute-start | bytes 786440 | tf_op jit(solution)/shard_map/ppermute | solution.py:239
  64.5 3.5 %collective-permute-done.2.refs_4_ = bf16[256,512]{1,0:T(8,128)(2,1)S(1)} collective-permute-done((bf16[256,512]{1,0:T(8,128)(2,1)S(1)}, bf16[256,512]{1,0:T(8,128)(2,1)S(1)}, u32[]{:S(2)}, u32[]{:S(2)}) %collective-permute-start.2) | collective-permute-done | bytes 262176 | tf_op jit(solution)/shard_map/ppermute | solution.py:239
  68.1 1.4 %collective-permute-done.3.refs_5_ = bf16[256,512]{1,0:T(8,128)(2,1)S(1)} collective-permute-done((bf16[256,512]{1,0:T(8,128)(2,1)S(1)}, bf16[256,512]{1,0:T(8,128)(2,1)S(1)}, u32[]{:S(2)}, u32[]{:S(2)}) %collective-permute-start.3) | collective-permute-done | bytes 262176 | tf_op jit(solution)/shard_map/ppermute | solution.py:239
  69.5 2.4 %collective-permute-done.5.refs_7_ = bf16[256,512]{1,0:T(8,128)(2,1)S(1)} collective-permute-done((bf16[256,512]{1,0:T(8,128)(2,1)S(1)}, bf16[256,512]{1,0:T(8,128)(2,1)S(1)}, u32[]{:S(2)}, u32[]{:S(2)}) %collective-permute-start.5) | collective-permute-done | bytes 262176 | tf_op jit(solution)/shard_map/ppermute | solution.py:239
  72.0 2.5 %collective-permute-done.6.refs_8_ = bf16[256,512]{1,0:T(8,128)(2,1)S(1)} collective-permute-done((bf16[256,512]{1,0:T(8,128)(2,1)S(1)}, bf16[256,512]{1,0:T(8,128)(2,1)S(1)}, u32[]{:S(2)}, u32[]{:S(2)}) %collective-permute-start.6) | collective-permute-done | bytes 262176 | tf_op jit(solution)/shard_map/ppermute | solution.py:239
  74.5 2.5 %norm.1 = bf16[256,4096]{1,0:T(8,128)(2,1)} custom-call(s32[1]{0:T(128)} %bitcast.refs_0_, f32[1,4096]{1,0:T(1,128)S(1)} %bitcast.7, bf16[256,512]{1,0:T(8,128)(2,1)S(1)} %collective-permute-done.refs_2_, bf16[256,512]{1,0:T(8,128)(2,1)S(1)} %collective-permute-done.1.refs_3_, bf16[256,512]{1,0:T(8,128)(2,1)S(1)} %collective-permute-done.2.refs_4_, ...), custom_call_target="tpu_custom_call" | custom-call | tf_op jit(solution)/shard_map/norm/pallas_call | solution.py:208
  (3 shorter events, 0.0 us)
Async XLA Ops:
  28.8 16.7 %all-to-all-start.1 = ((f32[32,16,128]{2,1,0:T(8,128)}), f32[32,16,128]{2,1,0:T(8,128)S(1)}, u32[]{:S(2)}, u32[]{:S(2)}) async-start(f32[32,16,128]{2,1,0:T(8,128)} %scan.1), calls=%async_computation.1 | async-start | bytes 524288 | tf_op jit(solution)/shard_map/all_to_all | solution.py:228
  47.1 14.2 %collective-permute-start = (bf16[256,512]{1,0:T(8,128)(2,1)S(1)}, bf16[256,512]{1,0:T(8,128)(2,1)S(1)}, u32[]{:S(2)}, u32[]{:S(2)}) collective-permute-start(bf16[256,512]{1,0:T(8,128)(2,1)S(1)} %carried.3), channel_id=1, source_target_pairs={{0,4},{1,5},{2,6},{3,7},{4,0},{5,1},{6,2},{7,3},{8,12},{9,13},{10,... | collective-permute-start | bytes 786440 | tf_op jit(solution)/shard_map/ppermute | solution.py:239
  52.0 22.5 %copy-start = (f32[4096]{0:T(1024)S(1)}, f32[4096]{0:T(1024)}, u32[]{:S(2)}) copy-start(f32[4096]{0:T(1024)} %param.7) | copy-start | bytes 49156
  52.0 11.7 %collective-permute-start.1 = (bf16[256,512]{1,0:T(8,128)(2,1)S(1)}, bf16[256,512]{1,0:T(8,128)(2,1)S(1)}, u32[]{:S(2)}, u32[]{:S(2)}) collective-permute-start(bf16[256,512]{1,0:T(8,128)(2,1)S(1)} %get-tuple-element.24), channel_id=1, source_target_pairs={{0,3},{1,4},{2,5},{3,6},{4,7},{5,0},{6,1},{7,2},{8,11},{9,12},{10,... | collective-permute-start | bytes 786440 | tf_op jit(solution)/shard_map/ppermute | solution.py:239
  58.2 9.9 %collective-permute-start.2 = (bf16[256,512]{1,0:T(8,128)(2,1)S(1)}, bf16[256,512]{1,0:T(8,128)(2,1)S(1)}, u32[]{:S(2)}, u32[]{:S(2)}) collective-permute-start(bf16[256,512]{1,0:T(8,128)(2,1)S(1)} %get-tuple-element.25), channel_id=1, source_target_pairs={{0,5},{1,6},{2,7},{3,0},{4,1},{5,2},{6,3},{7,4},{8,13},{9,14},{10,... | collective-permute-start | bytes 786440 | tf_op jit(solution)/shard_map/ppermute | solution.py:239
  58.6 10.9 %collective-permute-start.3 = (bf16[256,512]{1,0:T(8,128)(2,1)S(1)}, bf16[256,512]{1,0:T(8,128)(2,1)S(1)}, u32[]{:S(2)}, u32[]{:S(2)}) collective-permute-start(bf16[256,512]{1,0:T(8,128)(2,1)S(1)} %get-tuple-element.26), channel_id=1, source_target_pairs={{0,2},{1,3},{2,4},{3,5},{4,6},{5,7},{6,0},{7,1},{8,10},{9,11},{10,... | collective-permute-start | bytes 786440 | tf_op jit(solution)/shard_map/ppermute | solution.py:239
  59.6 10.0 %collective-permute-start.4 = (bf16[256,512]{1,0:T(8,128)(2,1)S(1)}, bf16[256,512]{1,0:T(8,128)(2,1)S(1)}, u32[]{:S(2)}, u32[]{:S(2)}) collective-permute-start(bf16[256,512]{1,0:T(8,128)(2,1)S(1)} %get-tuple-element.27), channel_id=1, source_target_pairs={{0,6},{1,7},{2,0},{3,1},{4,2},{5,3},{6,4},{7,5},{8,14},{9,15},{10,... | collective-permute-start | bytes 786440 | tf_op jit(solution)/shard_map/ppermute | solution.py:239
  61.3 10.7 %collective-permute-start.5 = (bf16[256,512]{1,0:T(8,128)(2,1)S(1)}, bf16[256,512]{1,0:T(8,128)(2,1)S(1)}, u32[]{:S(2)}, u32[]{:S(2)}) collective-permute-start(bf16[256,512]{1,0:T(8,128)(2,1)S(1)} %get-tuple-element.28), channel_id=1, source_target_pairs={{0,1},{1,2},{2,3},{3,4},{4,5},{5,6},{6,7},{7,0},{8,9},{9,10},{10,1... | collective-permute-start | bytes 786440 | tf_op jit(solution)/shard_map/ppermute | solution.py:239
  63.7 10.8 %collective-permute-start.6 = (bf16[256,512]{1,0:T(8,128)(2,1)S(1)}, bf16[256,512]{1,0:T(8,128)(2,1)S(1)}, u32[]{:S(2)}, u32[]{:S(2)}) collective-permute-start(bf16[256,512]{1,0:T(8,128)(2,1)S(1)} %get-tuple-element.29), channel_id=1, source_target_pairs={{0,7},{1,0},{2,1},{3,2},{4,3},{5,4},{6,5},{7,6},{8,15},{9,8},{10,9... | collective-permute-start | bytes 786440 | tf_op jit(solution)/shard_map/ppermute | solution.py:239
